TPU v7x, 256 devices: a whole 4x4x8 slice. The times are simulated.
256 devices in a mesh: space: 32 (over x, y, core), tm: 8 (over z).
Axes of the slice: x: 4, y: 4, z: 8, core: 2. Of those that a mesh axis runs over, the one named last changes fastest.
Arguments:
- velocity: bfloat16 [256, 2, 512, 1024], P('tm', None, 'space'), may hold values from -8.4 to 8.4
Outputs:
- vorticity: bfloat16 [256, 512, 1024], P('tm', 'space')
- modes: float32 [32, 512, 1024], P('tm', 'space')
All inputs are finite; a program needn't handle non-finite values.
Results may differ from a plain program's by a relative error of at most 0.003.
Values may be sent and summed in bfloat16 or wider, within the bound.
A program may use at most 64 MiB of HBM per device.

v0:
```python
import jax
import jax.numpy as jnp
from jax import lax
from jax.sharding import PartitionSpec as P

RANK = 32
HIGH = lax.Precision.HIGHEST


def halo_rows(block, width):
    count = lax.axis_size("space")
    forward = [(i, (i + 1) % count) for i in range(count)]
    backward = [(target, source) for source, target in forward]
    rows = block.shape[1]
    low = lax.ppermute(block[:, rows - width :], "space", forward)
    high = lax.ppermute(block[:, :width], "space", backward)
    return jnp.concatenate([low, block, high], axis=1)


def spanwise(field):
    ahead = jnp.roll(field, -1, 2)
    behind = jnp.roll(field, 1, 2)
    ahead_two = jnp.roll(field, -2, 2)
    behind_two = jnp.roll(field, 2, 2)
    return (8.0 * (ahead - behind) - (ahead_two - behind_two)) / 12.0


def merge_small(gram):
    coeffs = gram[:, :, :RANK] + gram[:, :, RANK:]
    diagonal = jnp.diagonal(gram, axis1=1, axis2=2)
    scales = jnp.sqrt(diagonal[:, :RANK] + diagonal[:, RANK:])
    half = jnp.einsum("nab,nbc->nac", gram, coeffs, precision=HIGH)
    inner = jnp.einsum("nab,nac->nbc", coeffs, half, precision=HIGH)
    lower = jnp.linalg.cholesky(inner)
    eye = jnp.broadcast_to(jnp.eye(RANK, dtype=jnp.float32), inner.shape)
    lower_inv = lax.linalg.triangular_solve(lower, eye, left_side=True, lower=True)
    factor = jnp.swapaxes(lower_inv, 1, 2) * scales[:, None, :]
    return jnp.einsum("nab,nbc->nac", coeffs, factor, precision=HIGH)


def tree_basis(gram, leaves):
    width = leaves * RANK
    basis = None
    span = 1
    while span < leaves:
        nodes = leaves // (2 * span)
        size = 2 * span * RANK
        sub = jnp.stack(
            [gram[k * size : (k + 1) * size, k * size : (k + 1) * size] for k in range(nodes)]
        )
        if basis is None:
            h = sub
        else:
            b = basis.reshape(nodes, 2, span * RANK, RANK)
            zero = jnp.zeros_like(b[:, 0])
            bd = jnp.concatenate(
                [
                    jnp.concatenate([b[:, 0], zero], axis=2),
                    jnp.concatenate([zero, b[:, 1]], axis=2),
                ],
                axis=1,
            )
            gb = jnp.einsum("nab,nbc->nac", sub, bd, precision=HIGH)
            h = jnp.einsum("nab,nac->nbc", bd, gb, precision=HIGH)
        c = merge_small(h)
        if basis is None:
            basis = c
        else:
            basis = jnp.einsum("nab,nbc->nac", bd, c, precision=HIGH)
        span *= 2
    return basis.reshape(width, RANK)


def local(velocity):
    rows = velocity.shape[2]
    span_v = halo_rows(velocity[:, 1], 2).astype(jnp.float32)
    stream_u = velocity[:, 0].astype(jnp.float32)
    dv_dx = (
        8.0 * (span_v[:, 3 : rows + 3] - span_v[:, 1 : rows + 1])
        - (span_v[:, 4:] - span_v[:, :rows])
    ) / 12.0
    vorticity = (dv_dx - spanwise(stream_u)).astype(jnp.bfloat16)
    blocks = lax.axis_size("tm")
    cells = lax.all_to_all(vorticity, "tm", 2, 0, tiled=True)
    flat = cells.reshape(cells.shape[0], -1)
    gram = jnp.einsum("ax,bx->ab", flat, flat, preferred_element_type=jnp.float32)
    gram = lax.psum(gram, ("space", "tm"))
    basis = tree_basis(gram, blocks)
    part = jnp.einsum("ab,ax->bx", basis, flat.astype(jnp.float32), precision=HIGH).reshape(
        RANK, rows, -1
    )
    modes = lax.all_to_all(part, "tm", 0, 2, tiled=True)
    return (vorticity, modes)


def solution(mesh):
    in_specs = (P("tm", None, "space", None),)
    out_specs = (P("tm", "space", None), P("tm", "space", None))
    return jax.shard_map(local, mesh=mesh, in_specs=in_specs, out_specs=out_specs, check_vma=False)
```

profile of v0, /device:TPU:2, one launch (start us, length us, event | category | flops | bytes accessed | tf_op | source)
XLA Modules:
  0.0 411.2 jit_solution(9131504356403751906)
XLA Ops:
  7.2 1.9 bitcast_convert_fusion
  9.7 3.8 collective-permute-start.1
  15.4 0.8 collective-permute-done
  17.2 2.2 fusion.3
  19.4 5.1 %copy.130 = bf16[32,16,1024]{0,1,2:T(8,128)(2,1)} copy(bf16[32,16,1024]{2,1,0:T(8,128)(2,1)S(1)} %fusion.3) | data formatting | bytes 2097152 | tf_op jit(solution)/shard_map/convert_element_type | solution.py:82
  24.5 7.8 %reshape.157 = bf16[8,2,32768]{2,1,0:T(2,128)(2,1)} reshape(bf16[1024,16,32]{2,1,0:T(8,128)(2,1)} %bitcast.133) | data formatting | bytes 2097152
  32.4 8.5 %all-to-all-start = ((bf16[8,2,32768]{2,1,0:T(2,128)(2,1)}), bf16[8,2,32768]{2,1,0:T(2,128)(2,1)S(1)}, u32[]{:S(2)}, u32[]{:S(2)}) async-start(bf16[8,2,32768]{2,1,0:T(2,128)(2,1)} %reshape.157), calls=%async_computation | async-start | bytes 2097152 | tf_op jit(solution)/shard_map/all_to_all | solution.py:84
  41.1 28.5 %all-to-all-done = bf16[8,2,32768]{2,1,0:T(2,128)(2,1)S(1)} async-done(((bf16[8,2,32768]{2,1,0:T(2,128)(2,1)}), bf16[8,2,32768]{2,1,0:T(2,128)(2,1)S(1)}, u32[]{:S(2)}, u32[]{:S(2)}) %all-to-all-start) | async-done | bytes 1048608 | tf_op jit(solution)/shard_map/all_to_all | solution.py:84
  69.6 4.5 %reshape.158 = bf16[1024,16,32]{2,1,0:T(8,128)(2,1)} reshape(bf16[8,2,32768]{2,1,0:T(2,128)(2,1)S(1)} %all-to-all-done) | data formatting | bytes 2097152
  74.1 5.4 %copy.131 = bf16[32,16,8,128]{3,1,0,2:T(8,128)(2,1)S(1)} copy(bf16[32,16,8,128]{0,1,3,2:T(8,128)(2,1)} %bitcast.132) | data formatting | bytes 2097152 | tf_op jit(solution)/shard_map/all_to_all | solution.py:84
  79.5 1.2 fusion.10
  82.2 244.6 %all-reduce.6.cloned.1.call-done = f32[256,256]{0,1:T(8,128)} async-done(((f32[256,256]{0,1:T(8,128)}), f32[256,256]{0,1:T(8,128)}) %all-reduce.6.cloned.1.call-update) | async-done | bytes 262160 | tf_op jit(solution)/shard_map/psum | solution.py:87
  326.8 0.9 slice_bitcast_fusion.7
  327.8 1.9 copy.137
  329.7 0.9 fusion.70
  330.6 1.5 gather_fusion
  332.0 0.8 copy.138
  332.9 1.1 fusion.69
  334.1 11.7 %custom-call.21 = f32[4,32,32]{2,1,0:T(8,128)S(1)} custom-call(f32[4,32,32]{2,1,0:T(8,128)S(1)} %fusion.19), custom_call_target="Cholesky" | custom-call | tf_op jit(solution)/shard_map/jit(cholesky)/cholesky | solution.py:34
  346.1 9.8 %custom-call.22 = f32[4,1,32,32]{2,3,1,0:T(8,128)S(1)} custom-call(f32[4,1,32,32]{3,2,1,0:T(8,128)S(1)} %select_bitcast_fusion), custom_call_target="InvertDiagBlocksLowerTriangular" | custom-call | tf_op jit(solution)/shard_map/triangular_solve | solution.py:36
  355.9 0.9 convolution_multiply_fusion
  357.8 1.9 copy.147
  360.5 1.5 gather_fusion.1
  362.0 0.8 copy.148
  362.9 0.9 fusion.66
  363.9 5.9 %custom-call.23 = f32[2,32,32]{2,1,0:T(8,128)S(1)} custom-call(f32[2,32,32]{2,1,0:T(8,128)S(1)} %fusion.32), custom_call_target="Cholesky" | custom-call | tf_op jit(solution)/shard_map/jit(cholesky)/cholesky | solution.py:34
  370.0 4.9 %custom-call.24 = f32[2,1,32,32]{2,3,1,0:T(8,128)S(1)} custom-call(f32[2,1,32,32]{3,2,1,0:T(8,128)S(1)} %select_bitcast_fusion.1), custom_call_target="InvertDiagBlocksLowerTriangular" | custom-call | tf_op jit(solution)/shard_map/triangular_solve | solution.py:36
  375.0 0.9 convolution_multiply_fusion.1
  378.1 2.9 custom-call.25
  382.3 2.4 custom-call.26
  385.4 1.0 fusion.76
  386.6 17.1 %all_to_all.33 = f32[32,16,128]{2,1,0:T(8,128)S(1)} all-to-all(f32[32,16,128]{2,1,0:T(8,128)S(1)} %copy.153), channel_id=1, replica_groups=mesh['space'=32,'tm'=8] {'tm'}, dimensions={0} | all-to-all | bytes 524288 | tf_op jit(solution)/shard_map/all_to_all | solution.py:92
  (61 shorter events, 12.6 us)
Async XLA Ops:
  9.6 6.6 %collective-permute-start = (bf16[32,2,1024]{2,0,1:T(8,128)(2,1)S(1)}, bf16[32,2,1024]{2,0,1:T(8,128)(2,1)S(1)}, u32[]{:S(2)}, u32[]{:S(2)}) collective-permute-start(bf16[32,2,1024]{2,0,1:T(8,128)(2,1)S(1)} %get-tuple-element.18), channel_id=1, source_target_pairs={{0,8},{8,16},{16,24},{24,32},{32,40},{40,48},{48,56},{56,64},{64,7... | collective-permute-start | bytes 393224 | tf_op jit(solution)/shard_map/ppermute | solution.py:15
  9.7 6.5 %collective-permute-start.1 = (bf16[32,2,1024]{2,0,1:T(8,128)(2,1)S(1)}, bf16[32,2,1024]{2,0,1:T(8,128)(2,1)S(1)}, u32[]{:S(2)}, u32[]{:S(2)}) collective-permute-start(bf16[32,2,1024]{2,0,1:T(8,128)(2,1)S(1)} %get-tuple-element.19), channel_id=1, source_target_pairs={{8,0},{16,8},{24,16},{32,24},{40,32},{48,40},{56,48},{64,56},{72,6... | collective-permute-start | bytes 393224 | tf_op jit(solution)/shard_map/ppermute | solution.py:16
  19.4 5.1 %copy-start = (bf16[32,16,1024]{2,1,0:T(8,128)(2,1)}, bf16[32,16,1024]{2,1,0:T(8,128)(2,1)S(1)}, u32[]{:S(2)}) copy-start(bf16[32,16,1024]{2,1,0:T(8,128)(2,1)S(1)} %fusion.3) | copy-start | bytes 3145732
  32.4 37.2 %all-to-all-start = ((bf16[8,2,32768]{2,1,0:T(2,128)(2,1)}), bf16[8,2,32768]{2,1,0:T(2,128)(2,1)S(1)}, u32[]{:S(2)}, u32[]{:S(2)}) async-start(bf16[8,2,32768]{2,1,0:T(2,128)(2,1)} %reshape.157), calls=%async_computation | async-start | bytes 2097152 | tf_op jit(solution)/shard_map/all_to_all | solution.py:84
  40.8 286.0 %all-reduce.6.cloned.1.call-start = ((), (), s32[]{:S(2)}) async-start(), calls=%async_computation.2 | async-start | bytes 524288 | tf_op jit(solution)/shard_map/psum | solution.py:87
  327.7 29.5 %copy-start.1 = (f32[256,256]{0,1:T(8,128)S(1)}, f32[256,256]{0,1:T(8,128)}, u32[]{:S(2)}) copy-start(f32[256,256]{0,1:T(8,128)} %all-reduce.6.cloned.1.call-done) | copy-start | bytes 786436
Sparse Core Ops, SparseCore 0:
  80.8 245.9 all-reduce.5
where the time goes:
time: 412 us; the launch traced here: 411 us
  waiting for transfers between devices  274 us (67%)
  other arithmetic  44.8 us (11%)
  local copies, waits for them, and re-layouts  37.9 us (9%)
  blocking collectives  17.1 us (4%)
  between operations  14.4 us (3%)
  starting transfers between devices  12.6 us (3%)
  matrix products  10.4 us (3%)
    psum x1, waiting for transfers between devices, local(): gram = lax.psum(gram, ('space', 'tm'))  245 us
    all_to_all x1, waiting for transfers between devices, local(): cells = lax.all_to_all(vorticity, 'tm', 2, 0, tiled=True)  28.5 us
    another operation x9, other arithmetic, merge_small(): lower = jnp.linalg.cholesky(inner)  21.5 us
    another operation x7, other arithmetic, merge_small(): lax.linalg.triangular_solve(lower, eye, left_side=True, lower=True)  18 us
    all_to_all x1, blocking collectives, local(): modes = lax.all_to_all(part, 'tm', 0, 2, tiled=True)  17.1 us
    unnamed x8, local copies, waits for them, and re-layouts  13.2 us
    all_to_all x1, starting transfers between devices, local(): cells = lax.all_to_all(vorticity, 'tm', 2, 0, tiled=True)  8.47 us
  transfers between devices with their start and end apart: 4, of which 3 were waited for; matrix products, arithmetic and copies ran while one was open for 1% of the time, Pallas kernels for 0%

commit v1 on v0

--- a/solution.py
+++ b/solution.py
@@ -5,6 +5,17 @@
 
 RANK = 32
 HIGH = lax.Precision.HIGHEST
+
+
+def cut_along(array, dim, count):
+    before, after = (array.shape[:dim], array.shape[dim + 1 :])
+    return jnp.moveaxis(array.reshape(*before, count, -1, *after), dim, 0)
+
+
+def in_order(blocks, dim):
+    shape = list(blocks.shape[1:])
+    shape[dim] *= blocks.shape[0]
+    return jnp.moveaxis(blocks, 0, dim).reshape(shape)
 
 
 def halo_rows(block, width):
@@ -81,7 +92,14 @@
     ) / 12.0
     vorticity = (dv_dx - spanwise(stream_u)).astype(jnp.bfloat16)
     blocks = lax.axis_size("tm")
-    cells = lax.all_to_all(vorticity, "tm", 2, 0, tiled=True)
+    count_2, mine = (lax.axis_size("tm"), lax.axis_index("tm"))
+    parts = cut_along(vorticity, 2, count_2)
+    outs = [parts[mine]]
+    for step in range(1, count_2):
+        sent = parts[mine ^ step]
+        outs.append(lax.ppermute(sent, "tm", [(i_2, i_2 ^ step) for i_2 in range(count_2)]))
+    parts = jnp.stack(outs)[mine ^ jnp.arange(count_2)]
+    cells = in_order(parts, 0)
     flat = cells.reshape(cells.shape[0], -1)
     gram = jnp.einsum("ax,bx->ab", flat, flat, preferred_element_type=jnp.float32)
     gram = lax.psum(gram, ("space", "tm"))

time: 412 us -> 400 us (0.971)
  waiting for transfers between devices: 274 us -> 259 us
  local copies, waits for them, and re-layouts: 37.9 us -> 24.5 us
  starting transfers between devices: 12.6 us -> 25.3 us
    all_to_all x1 -> x0, waiting for transfers between devices: 28.5 us -> none  [local(): cells = lax.all_to_all(vorticity, 'tm', 2, 0, tiled=True)]
    ppermute x0 -> x7, starting transfers between devices: none -> 21.4 us  [local(): lax.ppermute(sent, 'tm', [(i_2, i_2 ^ step) for i_2 in range(count_2)])]
    ppermute x0 -> x7, waiting for transfers between devices: none -> 12.3 us  [local(): lax.ppermute(sent, 'tm', [(i_2, i_2 ^ step) for i_2 in range(count_2)])]
    unnamed x8 -> x28, local copies, waits for them, and re-layouts: 13.2 us -> 1.37 us
    all_to_all x1 -> x0, starting transfers between devices: 8.47 us -> none  [local(): cells = lax.all_to_all(vorticity, 'tm', 2, 0, tiled=True)]
    all_to_all x1 -> x0, local copies, waits for them, and re-layouts: 5.35 us -> none  [local(): cells = lax.all_to_all(vorticity, 'tm', 2, 0, tiled=True)]
    convert_element_type x1 -> x0, local copies, waits for them, and re-layouts: 5.11 us -> none  [local(): vorticity = (dv_dx - spanwise(stream_u)).astype(jnp.bfloat16)]
  transfers between devices with their start and end apart: 4 -> 10, of which waited for: 3 -> 4; matrix products, arithmetic and copies ran while one was open for 1% -> 2% of each run, Pallas kernels for 0% -> 0%
where the time goes in v1:
time: 400 us; the launch traced here: 399 us
  waiting for transfers between devices  259 us (65%)
  other arithmetic  47.9 us (12%)
  starting transfers between devices  25.3 us (6%)
  local copies, waits for them, and re-layouts  24.5 us (6%)
  blocking collectives  17.1 us (4%)
  between operations  14.5 us (4%)
  matrix products  10.4 us (3%)
    psum x1, waiting for transfers between devices, local(): gram = lax.psum(gram, ('space', 'tm'))  247 us
    another operation x9, other arithmetic, merge_small(): lower = jnp.linalg.cholesky(inner)  21.5 us
    ppermute x7, starting transfers between devices, local(): lax.ppermute(sent, 'tm', [(i_2, i_2 ^ step) for i_2 in range(count_2)])  21.4 us
    another operation x7, other arithmetic, merge_small(): lax.linalg.triangular_solve(lower, eye, left_side=True, lower=True)  18 us
    all_to_all x1, blocking collectives, local(): modes = lax.all_to_all(part, 'tm', 0, 2, tiled=True)  17.1 us
    ppermute x7, waiting for transfers between devices, local(): lax.ppermute(sent, 'tm', [(i_2, i_2 ^ step) for i_2 in range(count_2)])  12.3 us
  transfers between devices with their start and end apart: 10, of which 4 were waited for; matrix products, arithmetic and copies ran while one was open for 2% of the time, Pallas kernels for 0%

profile of v1, /device:TPU:2, one launch (start us, length us, event | category | flops | bytes accessed | tf_op | source)
XLA Modules:
  0.0 399.0 jit_solution(8789973421365868783)
XLA Ops:
  7.2 1.9 bitcast_convert_fusion
  10.0 3.9 collective-permute-start.1
  13.9 2.2 fusion.73
  16.0 2.7 fusion.75
  21.6 1.7 maximum_convert_fusion
  23.9 3.3 fusion.3
  27.5 2.4 constant_dynamic-slice_fusion
  29.9 2.0 collective-permute-start.2
  31.9 3.4 collective-permute-start.3
  35.4 6.5 %collective-permute-start.5 = (bf16[32,16,128]{2,1,0:T(8,128)(2,1)S(1)}, bf16[32,16,128]{2,1,0:T(8,128)(2,1)S(1)}, u32[]{:S(2)}, u32[]{:S(2)}) collective-permute-start(bf16[32,16,128]{2,1,0:T(8,128)(2,1)S(1)} %bitcast.188), channel_id=1, source_target_pairs={{0,4},{1,5},{2,6},{3,7},{4,0},{5,1},{6,2},{7,3},{8,12},{9,13},{10,... | collective-permute-start | bytes 393224 | tf_op jit(solution)/shard_map/ppermute | solution.py:100
  42.1 4.7 %collective-permute-start.7 = (bf16[32,16,128]{2,1,0:T(8,128)(2,1)S(1)}, bf16[32,16,128]{2,1,0:T(8,128)(2,1)S(1)}, u32[]{:S(2)}, u32[]{:S(2)}) collective-permute-start(bf16[32,16,128]{2,1,0:T(8,128)(2,1)S(1)} %bitcast.186), channel_id=1, source_target_pairs={{0,6},{1,7},{2,4},{3,5},{4,2},{5,3},{6,0},{7,1},{8,14},{9,15},{10,... | collective-permute-start | bytes 393224 | tf_op jit(solution)/shard_map/ppermute | solution.py:100
  46.8 4.1 %collective-permute-done.3 = bf16[32,16,128]{2,1,0:T(8,128)(2,1)S(1)} collective-permute-done((bf16[32,16,128]{2,1,0:T(8,128)(2,1)S(1)}, bf16[32,16,128]{2,1,0:T(8,128)(2,1)S(1)}, u32[]{:S(2)}, u32[]{:S(2)}) %collective-permute-start.3) | collective-permute-done | bytes 131104 | tf_op jit(solution)/shard_map/ppermute | solution.py:100
  50.9 4.8 %collective-permute-start.8 = (bf16[32,16,128]{2,1,0:T(8,128)(2,1)S(1)}, bf16[32,16,128]{2,1,0:T(8,128)(2,1)S(1)}, u32[]{:S(2)}, u32[]{:S(2)}) collective-permute-start(bf16[32,16,128]{2,1,0:T(8,128)(2,1)S(1)} %bitcast.185), channel_id=1, source_target_pairs={{0,7},{1,6},{2,5},{3,4},{4,3},{5,2},{6,1},{7,0},{8,15},{9,14},{10,... | collective-permute-start | bytes 393224 | tf_op jit(solution)/shard_map/ppermute | solution.py:100
  55.7 4.2 %collective-permute-done.6 = bf16[32,16,128]{2,1,0:T(8,128)(2,1)S(1)} collective-permute-done((bf16[32,16,128]{2,1,0:T(8,128)(2,1)S(1)}, bf16[32,16,128]{2,1,0:T(8,128)(2,1)S(1)}, u32[]{:S(2)}, u32[]{:S(2)}) %collective-permute-start.6) | collective-permute-done | bytes 131104 | tf_op jit(solution)/shard_map/ppermute | solution.py:100
  60.0 4.0 collective-permute-done.8
  64.9 1.2 fusion.10
  67.6 247.0 %all-reduce.6.cloned.1.call-done = f32[256,256]{0,1:T(8,128)} async-done(((f32[256,256]{0,1:T(8,128)}), f32[256,256]{0,1:T(8,128)}) %all-reduce.6.cloned.1.call-update) | async-done | bytes 262160 | tf_op jit(solution)/shard_map/psum | solution.py:105
  315.5 1.9 copy.115
  318.3 1.5 gather_fusion.1
  320.7 1.1 fusion.70
  321.9 11.7 %custom-call.21 = f32[4,32,32]{2,1,0:T(8,128)S(1)} custom-call(f32[4,32,32]{2,1,0:T(8,128)S(1)} %fusion.19), custom_call_target="Cholesky" | custom-call | tf_op jit(solution)/shard_map/jit(cholesky)/cholesky | solution.py:45
  333.9 9.8 %custom-call.22 = f32[4,1,32,32]{2,3,1,0:T(8,128)S(1)} custom-call(f32[4,1,32,32]{3,2,1,0:T(8,128)S(1)} %select_bitcast_fusion), custom_call_target="InvertDiagBlocksLowerTriangular" | custom-call | tf_op jit(solution)/shard_map/triangular_solve | solution.py:47
  343.7 0.9 convolution_multiply_fusion
  345.6 1.9 copy.125
  348.3 1.5 gather_fusion.2
  350.7 0.9 fusion.67
  351.7 5.9 %custom-call.23 = f32[2,32,32]{2,1,0:T(8,128)S(1)} custom-call(f32[2,32,32]{2,1,0:T(8,128)S(1)} %fusion.32), custom_call_target="Cholesky" | custom-call | tf_op jit(solution)/shard_map/jit(cholesky)/cholesky | solution.py:45
  357.8 4.9 %custom-call.24 = f32[2,1,32,32]{2,3,1,0:T(8,128)S(1)} custom-call(f32[2,1,32,32]{3,2,1,0:T(8,128)S(1)} %select_bitcast_fusion.1), custom_call_target="InvertDiagBlocksLowerTriangular" | custom-call | tf_op jit(solution)/shard_map/triangular_solve | solution.py:47
  365.8 2.9 custom-call.25
  370.1 2.4 custom-call.26
  373.2 1.0 fusion.77
  374.3 17.1 %all_to_all.18 = f32[32,16,128]{2,1,0:T(8,128)S(1)} all-to-all(f32[32,16,128]{2,1,0:T(8,128)S(1)} %copy.131), channel_id=1, replica_groups=mesh['space'=32,'tm'=8] {'tm'}, dimensions={0} | all-to-all | bytes 524288 | tf_op jit(solution)/shard_map/all_to_all | solution.py:110
  (95 shorter events, 19.3 us)
Async XLA Ops:
  7.2 307.4 %all-reduce.6.cloned.1.call-start = ((), (), s32[]{:S(2)}) async-start(), calls=%async_computation.1 | async-start | bytes 524288 | tf_op jit(solution)/shard_map/psum | solution.py:105
  10.0 11.6 %collective-permute-start = (bf16[32,2,1024]{2,1,0:T(2,128)(2,1)}, bf16[32,2,1024]{2,1,0:T(2,128)(2,1)S(1)}, u32[]{:S(2)}, u32[]{:S(2)}) collective-permute-start(bf16[32,2,1024]{2,1,0:T(2,128)(2,1)} %get-tuple-element.20), channel_id=1, source_target_pairs={{0,8},{8,16},{16,24},{24,32},{32,40},{40,48},{48,56},{56,64},{64,7... | collective-permute-start | bytes 393224 | tf_op jit(solution)/shard_map/ppermute | solution.py:26
  10.0 11.6 %collective-permute-start.1 = (bf16[32,2,1024]{2,1,0:T(2,128)(2,1)}, bf16[32,2,1024]{2,1,0:T(2,128)(2,1)}, u32[]{:S(2)}, u32[]{:S(2)}) collective-permute-start(bf16[32,2,1024]{2,1,0:T(2,128)(2,1)} %get-tuple-element.21), channel_id=1, source_target_pairs={{8,0},{16,8},{24,16},{32,24},{40,32},{48,40},{56,48},{64,56},{72,6... | collective-permute-start | bytes 393224 | tf_op jit(solution)/shard_map/ppermute | solution.py:27
  21.6 1.7 copy-start
  21.6 2.3 copy-start.1
  21.6 2.3 copy-start.3
  27.2 2.7 copy-start.2
  29.9 12.2 %collective-permute-start.2 = (bf16[32,16,128]{2,1,0:T(8,128)(2,1)S(1)}, bf16[32,16,128]{2,1,0:T(8,128)(2,1)S(1)}, u32[]{:S(2)}, u32[]{:S(2)}) collective-permute-start(bf16[32,16,128]{2,1,0:T(8,128)(2,1)S(1)} %bitcast.191), channel_id=1, source_target_pairs={{0,1},{1,0},{2,3},{3,2},{4,5},{5,4},{6,7},{7,6},{8,9},{9,8},{10,11... | collective-permute-start | bytes 393224 | tf_op jit(solution)/shard_map/ppermute | solution.py:100
  31.9 18.9 %collective-permute-start.3 = (bf16[32,16,128]{2,1,0:T(8,128)(2,1)S(1)}, bf16[32,16,128]{2,1,0:T(8,128)(2,1)S(1)}, u32[]{:S(2)}, u32[]{:S(2)}) collective-permute-start(bf16[32,16,128]{2,1,0:T(8,128)(2,1)S(1)} %bitcast.190), channel_id=1, source_target_pairs={{0,2},{1,3},{2,0},{3,1},{4,6},{5,7},{6,4},{7,5},{8,10},{9,11},{10,... | collective-permute-start | bytes 393224 | tf_op jit(solution)/shard_map/ppermute | solution.py:100
  35.3 20.4 %collective-permute-start.4 = (bf16[32,16,128]{2,1,0:T(8,128)(2,1)S(1)}, bf16[32,16,128]{2,1,0:T(8,128)(2,1)S(1)}, u32[]{:S(2)}, u32[]{:S(2)}) collective-permute-start(bf16[32,16,128]{2,1,0:T(8,128)(2,1)S(1)} %bitcast.189), channel_id=1, source_target_pairs={{0,3},{1,2},{2,1},{3,0},{4,7},{5,6},{6,5},{7,4},{8,11},{9,10},{10,... | collective-permute-start | bytes 393224 | tf_op jit(solution)/shard_map/ppermute | solution.py:100
  35.4 20.3 %collective-permute-start.5 = (bf16[32,16,128]{2,1,0:T(8,128)(2,1)S(1)}, bf16[32,16,128]{2,1,0:T(8,128)(2,1)S(1)}, u32[]{:S(2)}, u32[]{:S(2)}) collective-permute-start(bf16[32,16,128]{2,1,0:T(8,128)(2,1)S(1)} %bitcast.188), channel_id=1, source_target_pairs={{0,4},{1,5},{2,6},{3,7},{4,0},{5,1},{6,2},{7,3},{8,12},{9,13},{10,... | collective-permute-start | bytes 393224 | tf_op jit(solution)/shard_map/ppermute | solution.py:100
  41.9 18.0 %collective-permute-start.6 = (bf16[32,16,128]{2,1,0:T(8,128)(2,1)S(1)}, bf16[32,16,128]{2,1,0:T(8,128)(2,1)S(1)}, u32[]{:S(2)}, u32[]{:S(2)}) collective-permute-start(bf16[32,16,128]{2,1,0:T(8,128)(2,1)S(1)} %bitcast.187), channel_id=1, source_target_pairs={{0,5},{1,4},{2,7},{3,6},{4,1},{5,0},{6,3},{7,2},{8,13},{9,12},{10,... | collective-permute-start | bytes 393224 | tf_op jit(solution)/shard_map/ppermute | solution.py:100
  42.1 17.9 %collective-permute-start.7 = (bf16[32,16,128]{2,1,0:T(8,128)(2,1)S(1)}, bf16[32,16,128]{2,1,0:T(8,128)(2,1)S(1)}, u32[]{:S(2)}, u32[]{:S(2)}) collective-permute-start(bf16[32,16,128]{2,1,0:T(8,128)(2,1)S(1)} %bitcast.186), channel_id=1, source_target_pairs={{0,6},{1,7},{2,4},{3,5},{4,2},{5,3},{6,0},{7,1},{8,14},{9,15},{10,... | collective-permute-start | bytes 393224 | tf_op jit(solution)/shard_map/ppermute | solution.py:100
  50.9 13.1 %collective-permute-start.8 = (bf16[32,16,128]{2,1,0:T(8,128)(2,1)S(1)}, bf16[32,16,128]{2,1,0:T(8,128)(2,1)S(1)}, u32[]{:S(2)}, u32[]{:S(2)}) collective-permute-start(bf16[32,16,128]{2,1,0:T(8,128)(2,1)S(1)} %bitcast.185), channel_id=1, source_target_pairs={{0,7},{1,6},{2,5},{3,4},{4,3},{5,2},{6,1},{7,0},{8,15},{9,14},{10,... | collective-permute-start | bytes 393224 | tf_op jit(solution)/shard_map/ppermute | solution.py:100
  67.6 266.0 %copy-start.5 = (pred[32,32]{1,0:T(8,128)(4,1)S(1)}, pred[32,32]{1,0:T(8,128)(4,1)}, u32[]{:S(2)}) copy-start(pred[32,32]{1,0:T(8,128)(4,1)} %iota_compare_fusion.7) | copy-start | bytes 3076
  315.5 29.5 %copy-start.4 = (f32[256,256]{0,1:T(8,128)S(1)}, f32[256,256]{0,1:T(8,128)}, u32[]{:S(2)}) copy-start(f32[256,256]{0,1:T(8,128)} %all-reduce.6.cloned.1.call-done) | copy-start | bytes 786436
Sparse Core Ops, SparseCore 0:
  66.2 248.3 all-reduce.5
